TPU v7x, 32 devices: a whole 2x2x4 slice. The times are simulated.
32 devices in a mesh: gx: 8 (over y, x, core), gy: 4 (over z).
Axes of the slice: x: 2, y: 2, z: 4, core: 2. Of those that a mesh axis runs over, the one named last changes fastest.
Arguments:
- positions: float32 [3, 8, 4, 128], P(None, 'gx', 'gy'), may hold values from 0 to 384, as said below
- neighbours: int32 [32, 8, 4, 128], P(None, 'gx', 'gy'), may hold values from 0 to 1151, as said below
- live_count: int32 [8, 4], P('gx', 'gy'), may hold values from 16 to 128, as said below
- stencil_base: int32 [3, 8, 4, 128], P(None, 'gx', 'gy'), may hold values from -1 to 383, as said below
- spline_weight: float32 [3, 4, 8, 4, 128], P(None, None, 'gx', 'gy'), may hold values from 0 to 1, as said below
- spline_slope: float32 [3, 4, 8, 4, 128], P(None, None, 'gx', 'gy'), may hold values from -1 to 1, as said below
- embed_scale: float32 [100], replicated, may hold values from -12 to 12
- embed_bias: float32 [100], replicated, may hold values from -4 to 4
- desc_gain: float32 [1600], replicated, may hold values from 0.25 to 1.75
- fit_in: bfloat16 [128, 1600], replicated, may hold values from -0.15625 to 0.15625
- fit_bias: float32 [128], replicated, may hold values from -3 to 3
- fit_hidden: bfloat16 [128, 128], replicated, may hold values from -0.5 to 0.5
- fit_bias_two: float32 [128], replicated, may hold values from -3 to 3
- fit_out: float32 [128], replicated, may hold values from -0.5 to 0.5
Outputs:
- centroid_energy: float32 [8, 4, 128], P('gx', 'gy')
- centroid_force: float32 [3, 8, 4, 128], P(None, 'gx', 'gy')
Inputs may be any that keep to these rules, and one draw needn't show every extreme that they name: `live_count`: slots below a column's count are live; some column has all 128 slots live. `neighbours`: every entry names a live slot of one of the nine blocks of the column's neighbourhood. `stencil_base`: along x the base lies in -1 to 46, along y in -1 to 94, along z in 0 to 383. `positions`: x lies in 0 to 48, y in 0 to 96, z in 0 to 384. `spline_weight`: cubic B-spline weights of a fraction in [0, 1) for each axis; the four weights sum to one. `spline_slope`: the derivatives of those weights with respect to the fraction.
All inputs are finite; a program needn't handle non-finite values.
Results may differ from a plain program's by a relative error of at most 0.006.
The roundings to bfloat16 on the way count: a program that leaves them out, or rounds other values in their place, can miss the bound.
Values sent between devices are 32-bit elements; how exact they have to be, the bound alone decides.
A program may use at most 128 MiB of HBM per device.

v0:
```python
import math

import jax
import jax.numpy as jnp
from jax import lax
from jax.sharding import PartitionSpec as P

GRID = 384
AXIS = 16


highest = lax.Precision.HIGHEST
radius_scale = 4.0
screen_width = 0.25
norm_floor = 1e-06
full_turn = 2.0 * math.pi


def padded_2(shard, sides, width):
    for axis, dim in sides:
        peers, length = (lax.axis_size(axis), shard.shape[dim])
        up = [(i, (i + 1) % peers) for i in range(peers)]
        down = [(j, i) for i, j in up]
        last = lax.slice_in_dim(shard, length - width, length, axis=dim)
        leading = lax.slice_in_dim(shard, 0, width, axis=dim)
        before = lax.ppermute(last, axis, up)
        after = lax.ppermute(leading, axis, down)
        shard = jnp.concatenate([before, shard, after], axis=dim)
    return shard


def shifted(block, axis, distance):
    devices = range(lax.axis_size(axis))
    route = [((i - distance) % len(devices), i) for i in devices]
    return lax.ppermute(block, axis, route)


def stencil_table(anchor, weights, length, offset, periodic):
    count = anchor.shape[0]
    cell_index = lax.broadcasted_iota(jnp.int32, (4, length, count), 1)
    tap_index = lax.broadcasted_iota(jnp.int32, (4, length, count), 0)
    target = anchor[None, None, :] + tap_index + offset
    if periodic:
        target = target % length
    chosen = jnp.where(target == cell_index, weights[:, None, :], jnp.zeros((), weights.dtype))
    return jnp.sum(chosen, axis=0)


def spread_cells(charge, anchor, weights, extent_x, extent_y, offset, length):
    table_x = stencil_table(anchor[0], weights[0] * charge[None, :], extent_x, offset, False)
    table_y = stencil_table(anchor[1], weights[1], extent_y, offset, False)
    table_z = stencil_table(anchor[2], weights[2], length, 0, True)
    planes = (table_x[:, None, :] * table_y[None, :, :]).reshape(extent_x * extent_y, -1)
    return jnp.dot(planes, table_z.T, precision=highest).reshape(extent_x, extent_y, length)


def interpolate(padded, anchor, weights, slopes):
    extent_x, extent_y, length = padded.shape
    table_x = stencil_table(anchor[0], weights[0], extent_x, 2, False)
    slope_x = stencil_table(anchor[0], slopes[0], extent_x, 2, False)
    table_y = stencil_table(anchor[1], weights[1], extent_y, 2, False)
    slope_y = stencil_table(anchor[1], slopes[1], extent_y, 2, False)
    table_z = stencil_table(anchor[2], weights[2], length, 0, True)
    slope_z = stencil_table(anchor[2], slopes[2], length, 0, True)
    flat = padded.reshape(extent_x * extent_y, length)
    along = jnp.dot(flat, table_z, precision=highest).reshape(extent_x, extent_y, -1)
    slant = jnp.dot(flat, slope_z, precision=highest).reshape(extent_x, extent_y, -1)
    over_y = jnp.sum(along * table_y[None], axis=1)
    value = jnp.sum(table_x * over_y, axis=0)
    field_x = -jnp.sum(slope_x * over_y, axis=0)
    over_x = jnp.sum(along * table_x[:, None, :], axis=0)
    field_y = -jnp.sum(slope_y * over_x, axis=0)
    slant_y = jnp.sum(slant * table_y[None], axis=1)
    field_z = -jnp.sum(table_x * slant_y, axis=0)
    return (value, jnp.stack([field_x, field_y, field_z]))


def fitted_charge(
    nearby,
    listed,
    count,
    embed_scale,
    embed_bias,
    desc_gain,
    fit_in,
    fit_bias,
    fit_hidden,
    fit_bias_two,
    fit_out,
):
    atoms = listed.shape[1]
    center = nearby[:, 4 * atoms : 5 * atoms]
    picked = jnp.take(nearby, listed.reshape(-1), axis=1).reshape(3, listed.shape[0], atoms)
    delta = picked - center[:, None, :]
    radius = jnp.sqrt(jnp.sum(delta * delta, axis=0))
    smooth = 1.0 / (1.0 + radius / radius_scale)
    factor = smooth / (radius + radius_scale)
    envelope = jnp.concatenate([smooth[None], delta * factor[None]], axis=0)
    embed = jnp.tanh(smooth[None] * embed_scale[:, None, None] + embed_bias[:, None, None])
    mixed = jnp.einsum("ekn,ckn->ecn", embed, envelope, precision=highest)
    descriptor = jnp.einsum("ecn,acn->ean", mixed, mixed[:AXIS], precision=highest).reshape(
        -1, atoms
    )
    scaling = lax.rsqrt(jnp.mean(descriptor * descriptor, axis=0) + norm_floor)
    normed = (descriptor * scaling[None, :] * desc_gain[:, None]).astype(jnp.bfloat16)
    first = jnp.tanh(
        jnp.dot(fit_in, normed, preferred_element_type=jnp.float32) + fit_bias[:, None]
    )
    second = (
        jnp.tanh(
            jnp.dot(fit_hidden, first.astype(jnp.bfloat16), preferred_element_type=jnp.float32)
            + fit_bias_two[:, None]
        )
        + first
    )
    charge = jnp.sum(fit_out[:, None] * second, axis=0)
    slot_index = lax.broadcasted_iota(jnp.int32, (atoms,), 0)
    return jnp.where(slot_index < count, charge, jnp.zeros((), charge.dtype))


def wave_number(index, length):
    signed = jnp.where(index > length // 2, index - length, index)
    return signed.astype(jnp.float32) * (full_turn / length)


def green_values(index_x, index_y, index_z, length):
    wave_x = wave_number(index_x, length)
    wave_y = wave_number(index_y, length)
    wave_z = wave_number(index_z, length)
    square = wave_x * wave_x + wave_y * wave_y + wave_z * wave_z
    safe = jnp.where(square > 0, square, 1.0)
    value = 2.0 * full_turn * jnp.exp(-0.5 * screen_width * screen_width * square) / safe
    keep = (square > 0) & (index_z != length // 2)
    return jnp.where(keep, value, 0.0)


def wave_tables(length, count):
    rows = lax.broadcasted_iota(jnp.int32, (length, count), 0)
    cols = lax.broadcasted_iota(jnp.int32, (length, count), 1)
    angle = (rows * cols % length).astype(jnp.float32) * (full_turn / length)
    return (jnp.cos(angle), jnp.sin(angle))


def along_axis(real_part, imag_part, cosine, sine, sign, form):
    real_cos = jnp.einsum(form, real_part, cosine, precision=highest)
    real_sin = jnp.einsum(form, real_part, sine, precision=highest)
    imag_cos = jnp.einsum(form, imag_part, cosine, precision=highest)
    imag_sin = jnp.einsum(form, imag_part, sine, precision=highest)
    return (real_cos + sign * imag_sin, imag_cos - sign * real_sin)


def local(
    positions,
    neighbours,
    live_count,
    stencil_base,
    spline_weight,
    spline_slope,
    embed_scale,
    embed_bias,
    desc_gain,
    fit_in,
    fit_bias,
    fit_hidden,
    fit_bias_two,
    fit_out,
):
    columns_y = lax.axis_size("gy")
    width_x = GRID // lax.axis_size("gx")
    width_y = GRID // columns_y
    atoms = positions.shape[3]
    beside_all = padded_2(positions, (("gx", 1), ("gy", 2)), 1)
    block_x = lax.broadcasted_iota(jnp.int32, (3, 3, atoms), 0) - 1
    block_y = lax.broadcasted_iota(jnp.int32, (3, 3, atoms), 1) - 1
    offsets = jnp.stack([block_x * width_x, block_y * width_y, jnp.zeros_like(block_x)]).astype(
        jnp.float32
    )
    nearby = (beside_all + offsets).reshape(3, 9 * atoms)
    charge = fitted_charge(
        nearby,
        neighbours[:, 0, 0, :],
        live_count[0, 0],
        embed_scale,
        embed_bias,
        desc_gain,
        fit_in,
        fit_bias,
        fit_hidden,
        fit_bias_two,
        fit_out,
    )
    anchor = stencil_base[:, 0, 0, :]
    weights = spline_weight[:, :, 0, 0, :]
    slopes = spline_slope[:, :, 0, 0, :]
    spread = spread_cells(charge, anchor, weights, width_x + 4, width_y + 4, 2, GRID)
    inner = spread[2 : width_x + 2]
    for stride in (1, -1):
        piece = spread[width_x + 2 :] if stride == 1 else spread[:2]
        moved = shifted(piece, "gx", stride)
        if stride == 1:
            inner = inner.at[:2].add(moved)
        else:
            inner = inner.at[width_x - 2 :].add(moved)
    density = inner[:, 2 : width_y + 2]
    for stride in (1, -1):
        piece = inner[:, width_y + 2 :] if stride == 1 else inner[:, :2]
        moved = shifted(piece, "gy", stride)
        if stride == 1:
            density = density.at[:, :2].add(moved)
        else:
            density = density.at[:, width_y - 2 :].add(moved)
    freqs = GRID // 2
    fold_weight = jnp.where(jnp.arange(freqs) == 0, 1.0, 2.0).astype(jnp.float32) / GRID
    cosine_z, sine_z = wave_tables(GRID, freqs)
    flat = density.reshape(width_x * width_y, GRID)
    real_part = jnp.dot(flat, cosine_z, precision=highest).reshape(width_x, width_y, freqs)
    imag_part = -jnp.dot(flat, sine_z, precision=highest).reshape(width_x, width_y, freqs)
    real_part, imag_part = (
        lax.all_to_all(real_part, "gy", split_axis=2, concat_axis=1, tiled=True),
        lax.all_to_all(imag_part, "gy", split_axis=2, concat_axis=1, tiled=True),
    )
    cosine, sine = wave_tables(GRID, GRID)
    real_part, imag_part = along_axis(real_part, imag_part, cosine, sine, 1.0, "xym,yk->xkm")
    real_part, imag_part = (
        lax.all_to_all(real_part, "gx", split_axis=1, concat_axis=0, tiled=True),
        lax.all_to_all(imag_part, "gx", split_axis=1, concat_axis=0, tiled=True),
    )
    real_part, imag_part = along_axis(real_part, imag_part, cosine, sine, 1.0, "xym,xk->kym")
    span_y = real_part.shape[1]
    span_z = real_part.shape[2]
    index_x = lax.broadcasted_iota(jnp.int32, (GRID, span_y, span_z), 0)
    index_y = lax.axis_index("gx") * span_y + lax.broadcasted_iota(
        jnp.int32, (GRID, span_y, span_z), 1
    )
    index_z = lax.axis_index("gy") * span_z + lax.broadcasted_iota(
        jnp.int32, (GRID, span_y, span_z), 2
    )
    green = green_values(index_x, index_y, index_z, GRID)
    real_part = real_part * green
    imag_part = imag_part * green
    back_cos = cosine / GRID
    back_sin = sine / GRID
    real_part, imag_part = along_axis(real_part, imag_part, back_cos, back_sin, -1.0, "xym,xk->kym")
    real_part, imag_part = (
        lax.all_to_all(real_part, "gx", split_axis=0, concat_axis=1, tiled=True),
        lax.all_to_all(imag_part, "gx", split_axis=0, concat_axis=1, tiled=True),
    )
    real_part, imag_part = along_axis(real_part, imag_part, back_cos, back_sin, -1.0, "xym,yk->xkm")
    real_part, imag_part = (
        lax.all_to_all(real_part, "gy", split_axis=1, concat_axis=2, tiled=True),
        lax.all_to_all(imag_part, "gy", split_axis=1, concat_axis=2, tiled=True),
    )
    rows_y = real_part.shape[1]
    flat_real = real_part.reshape(width_x * rows_y, freqs)
    flat_imag = imag_part.reshape(width_x * rows_y, freqs)
    summed_cos = (cosine_z * fold_weight[None, :]).T
    summed_sin = (sine_z * fold_weight[None, :]).T
    potential = jnp.dot(flat_real, summed_cos, precision=highest) - jnp.dot(
        flat_imag, summed_sin, precision=highest
    )
    potential = potential.reshape(width_x, rows_y, GRID)
    padded = padded_2(potential, (("gx", 0), ("gy", 1)), 2)
    value, field = interpolate(padded, anchor, weights, slopes)
    energy = (0.5 * charge * value).reshape(1, 1, atoms)
    force = (charge[None, :] * field).reshape(3, 1, 1, atoms)
    return (energy, force)


def solution(mesh):
    placed = (
        P(None, "gx", "gy", None),
        P(None, "gx", "gy", None),
        P("gx", "gy"),
        P(None, "gx", "gy", None),
        P(None, None, "gx", "gy", None),
        P(None, None, "gx", "gy", None),
        P(),
        P(),
        P(),
        P(),
        P(),
        P(),
        P(),
        P(),
    )
    return jax.shard_map(
        local,
        mesh=mesh,
        in_specs=placed,
        out_specs=(P("gx", "gy", None), P(None, "gx", "gy", None)),
        check_vma=False,
    )
```

profile of v0, /device:TPU:0, one launch (start us, length us, event | category | flops | bytes accessed | tf_op | source)
XLA Modules:
  0.0 1188.1 jit_solution(777456584201518646)
XLA Ops:
  20.5 14.2 %gather_fusion = f32[4096,3]{1,0:T(8,128)} fusion(f32[3,1152]{0,1:T(8,128)S(1)} %bitcast_add_fusion, s32[4096]{0:T(1024)S(1)} %broadcast_clamp_fusion), kind=kCustom, calls=%fused_computation | custom fusion | bytes 114688 | tf_op jit(solution)/shard_map/jit(_take)/gather | solution.py:93
  94.5 11.3 convolution_negate_fusion
  118.0 13.0 %fusion.70 = f32[48,96,192]{2,1,0:T(8,128)} fusion(f32[48,96,384]{2,1,0:T(8,128)} %copy-done.2), kind=kOutput, calls=%fused_computation.86 | convolution fusion | flops 4077527040 | bytes 10616832 | tf_op jit(solution)/shard_map/dot_general | solution.py:216
  137.7 82.3 %all-to-all-done.1 = f32[48,96,192]{1,0,2:T(8,128)} async-done(((f32[48,96,192]{1,0,2:T(8,128)}), f32[48,96,192]{1,0,2:T(8,128)}, u32[]{:S(2)}, u32[]{:S(2)}) %all-to-all-start.1) | async-done | bytes 3538976 | tf_op jit(solution)/shard_map/all_to_all | solution.py:220
  238.6 90.8 %all-to-all-done = f32[48,96,192]{1,0,2:T(8,128)} async-done(((f32[48,96,192]{1,0,2:T(8,128)}), f32[48,96,192]{1,0,2:T(8,128)}, u32[]{:S(2)}, u32[]{:S(2)}) %all-to-all-start) | async-done | bytes 3538976 | tf_op jit(solution)/shard_map/all_to_all | solution.py:219
  342.8 11.4 fusion.37
  354.2 9.5 fusion.47
  373.7 12.1 %reshape.515 = f32[8,1,110592]{2,1,0:T(1,128)} reshape(f32[384,48,48]{2,1,0:T(8,128)} %bitcast.215) | data formatting | bytes 7077888
  390.7 11.4 fusion.33
  402.0 9.4 fusion.45
  421.4 12.1 %reshape.517 = f32[8,1,110592]{2,1,0:T(1,128)} reshape(f32[384,48,48]{2,1,0:T(8,128)} %bitcast.216) | data formatting | bytes 7077888
  438.9 39.4 %reduce.14 = f32[8,110592]{1,0:T(8,128)} reduce(f32[8,1,110592]{2,1,0:T(1,128)} %all-to-all-done.2, f32[]{:T(128)} %broadcast.468), dimensions={1}, to_apply=%all_to_all.108.reduce_sub_computation | reduce | bytes 7077892 | tf_op jit(solution)/shard_map/all_to_all | solution.py:225
  478.3 9.4 reshape.516
  487.7 9.6 copy.112
  505.6 14.6 %fusion.40 = f32[384,2304]{0,1} fusion(f32[384,2304]{0,1:T(8,128)} %reshape.480), kind=kOutput, calls=%fused_computation.65 | convolution fusion | flops 4078190592 | bytes 7077888
  520.1 10.4 fusion.35
  530.5 39.6 %reduce.13 = f32[8,110592]{1,0:T(8,128)} reduce(f32[8,1,110592]{2,1,0:T(1,128)} %all-to-all-done.3, f32[]{:T(128)} %broadcast.468), dimensions={1}, to_apply=%all_to_all.112.reduce_sub_computation | reduce | bytes 7077892 | tf_op jit(solution)/shard_map/all_to_all | solution.py:226
  570.1 9.4 reshape.518
  579.5 9.6 copy.114
  597.6 11.4 fusion.31
  609.0 9.7 fusion.43
  622.9 9.4 fusion.64
  632.3 9.6 fusion.56
  651.9 12.1 %reshape.519 = f32[8,1,110592]{2,1,0:T(1,128)} reshape(f32[384,48,48]{2,1,0:T(8,128)} %copy.115) | data formatting | bytes 7077888
  668.9 11.5 fusion.60
  680.4 9.5 fusion.54
  699.9 12.1 %reshape.521 = f32[8,1,110592]{2,1,0:T(1,128)} reshape(f32[384,48,48]{2,1,0:T(8,128)} %copy.117) | data formatting | bytes 7077888
  716.7 39.4 %reduce.15 = f32[8,110592]{1,0:T(8,128)} reduce(f32[8,1,110592]{2,1,0:T(1,128)} %all-to-all-done.4, f32[]{:T(128)} %broadcast.468), dimensions={1}, to_apply=%all_to_all.116.reduce_sub_computation | reduce | bytes 7077892 | tf_op jit(solution)/shard_map/all_to_all | solution.py:245
  756.1 9.4 reshape.520
  765.6 9.6 copy.116
  783.4 14.1 %fusion.62 = f32[384,2304]{0,1} fusion(f32[384,2304]{0,1:T(8,128)} %bitcast.229), kind=kOutput, calls=%fused_computation.77 | convolution fusion | flops 4078338048 | bytes 7077888
  797.5 39.4 %reduce.16 = f32[8,110592]{1,0:T(8,128)} reduce(f32[8,1,110592]{2,1,0:T(1,128)} %all-to-all-done.5, f32[]{:T(128)} %broadcast.468), dimensions={1}, to_apply=%all_to_all.120.reduce_sub_computation | reduce | bytes 7077892 | tf_op jit(solution)/shard_map/all_to_all | solution.py:246
  836.9 9.4 reshape.522
  846.4 9.6 copy.118
  864.4 11.5 fusion.52
  885.9 11.5 reshape.523
  902.4 11.5 fusion.58
  913.8 9.8 fusion.50
  933.6 11.5 reshape.525
  945.1 37.1 %all-to-all-done.6 = f32[4,1,221184]{2,1,0:T(1,128)} async-done(((f32[4,1,221184]{2,1,0:T(1,128)}), f32[4,1,221184]{2,1,0:T(1,128)}, u32[]{:S(2)}, u32[]{:S(2)}) %all-to-all-start.6) | async-done | bytes 3538976 | tf_op jit(solution)/shard_map/all_to_all | solution.py:250
  987.1 40.4 %reduce.17 = f32[4,221184]{1,0:T(4,128)} reduce(f32[4,1,221184]{2,1,0:T(1,128)} %all-to-all-done.6, f32[]{:T(128)} %broadcast.468), dimensions={1}, to_apply=%all_to_all.124.reduce_sub_computation | reduce | bytes 7077892 | tf_op jit(solution)/shard_map/all_to_all | solution.py:250
  1027.5 10.0 reshape.524
  1037.5 9.0 copy.120
  1052.3 14.0 %all-to-all-done.7 = f32[4,1,221184]{2,1,0:T(1,128)} async-done(((f32[4,1,221184]{2,1,0:T(1,128)}), f32[4,1,221184]{2,1,0:T(1,128)}, u32[]{:S(2)}, u32[]{:S(2)}) %all-to-all-start.7) | async-done | bytes 3538976 | tf_op jit(solution)/shard_map/all_to_all | solution.py:251
  1066.3 40.7 %reduce.18 = f32[4,221184]{1,0:T(4,128)} reduce(f32[4,1,221184]{2,1,0:T(1,128)} %all-to-all-done.7, f32[]{:T(128)} %broadcast.468), dimensions={1}, to_apply=%all_to_all.127.reduce_sub_computation | reduce | bytes 7077892 | tf_op jit(solution)/shard_map/all_to_all | solution.py:251
  1107.0 10.0 reshape.526
  1117.0 9.0 copy.122
  1132.2 11.1 fusion.73
  (210 shorter events, 313.1 us)
Async XLA Ops:
  0.6 42.8 %copy-start = (bf16[128,1600]{0,1:T(8,128)(2,1)S(1)}, bf16[128,1600]{0,1:T(8,128)(2,1)}, u32[]{:S(2)}) copy-start(bf16[128,1600]{0,1:T(8,128)(2,1)} %param.31) | copy-start | bytes 1228804
  0.6 9.0 collective-permute-start
  1.2 9.2 collective-permute-start.1
  9.6 39.7 %copy-start.16 = (f32[384,128]{1,0:T(8,128)}, f32[384,128]{1,0:T(8,128)S(1)}, u32[]{:S(2)}) copy-start(f32[384,128]{1,0:T(8,128)S(1)} %get-tuple-element.61) | copy-start | bytes 589828
  9.6 27.8 %copy-start.31 = (f32[100]{0:T(128)S(1)}, f32[100]{0:T(128)}, u32[]{:S(2)}) copy-start(f32[100]{0:T(128)} %param.29) | copy-start | bytes 1204
  9.6 27.8 %copy-start.32 = (f32[100]{0:T(128)S(1)}, f32[100]{0:T(128)}, u32[]{:S(2)}) copy-start(f32[100]{0:T(128)} %param.28) | copy-start | bytes 1204
  10.4 6.1 collective-permute-start.3
  14.8 5.4 collective-permute-start.2
  15.6 29.3 %copy-start.19 = (f32[100,128]{1,0:T(8,128)}, f32[100,128]{1,0:T(8,128)S(1)}, u32[]{:S(2)}) copy-start(f32[100,128]{1,0:T(8,128)S(1)} %get-tuple-element.59) | copy-start | bytes 153604
  37.4 6.4 copy-start.30
  37.5 6.4 copy-start.33
  59.9 17.0 %collective-permute-start.4 = (f32[2,100,384]{2,1,0:T(8,128)S(1)}, f32[2,100,384]{2,1,0:T(8,128)S(1)}, u32[]{:S(2)}, u32[]{:S(2)}) collective-permute-start(f32[2,100,384]{2,1,0:T(8,128)S(1)} %slice.207), channel_id=1, source_target_pairs={{28,0},{0,4},{4,8},{8,12},{12,16},{16,20},{20,24},{24,28},{29,1},{... | collective-permute-start | bytes 921608 | tf_op jit(solution)/shard_map/ppermute | solution.py:35
  60.0 17.7 %collective-permute-start.5 = (f32[2,100,384]{2,1,0:T(8,128)S(1)}, f32[2,100,384]{2,1,0:T(8,128)S(1)}, u32[]{:S(2)}, u32[]{:S(2)}) collective-permute-start(f32[2,100,384]{2,1,0:T(8,128)S(1)} %slice.210), channel_id=1, source_target_pairs={{4,0},{8,4},{12,8},{16,12},{20,16},{24,20},{28,24},{0,28},{5,1},{9... | collective-permute-start | bytes 921608 | tf_op jit(solution)/shard_map/ppermute | solution.py:35
  80.8 8.0 collective-permute-start.6
  84.9 6.5 collective-permute-start.7
  112.5 107.6 %all-to-all-start.1 = ((f32[48,96,192]{1,0,2:T(8,128)}), f32[48,96,192]{1,0,2:T(8,128)}, u32[]{:S(2)}, u32[]{:S(2)}) async-start(f32[48,96,192]{1,0,2:T(8,128)} %copy.108), calls=%async_computation.1 | async-start | bytes 9437184 | tf_op jit(solution)/shard_map/all_to_all | solution.py:220
  220.0 109.4 %all-to-all-start = ((f32[48,96,192]{1,0,2:T(8,128)}), f32[48,96,192]{1,0,2:T(8,128)}, u32[]{:S(2)}, u32[]{:S(2)}) async-start(f32[48,96,192]{1,0,2:T(8,128)} %copy.105), calls=%async_computation | async-start | bytes 9437184 | tf_op jit(solution)/shard_map/all_to_all | solution.py:219
  342.8 11.4 copy-start.5
  385.8 47.8 %all-to-all-start.2 = ((f32[8,1,110592]{2,1,0:T(1,128)}), f32[8,1,110592]{2,1,0:T(1,128)}, u32[]{:S(2)}, u32[]{:S(2)}) async-start(f32[8,1,110592]{2,1,0:T(1,128)} %reshape.515), calls=%async_computation.2 | async-start | bytes 7077888 | tf_op jit(solution)/shard_map/all_to_all | solution.py:225
  390.6 11.4 copy-start.6
  433.5 97.0 %all-to-all-start.3 = ((f32[8,1,110592]{2,1,0:T(1,128)}), f32[8,1,110592]{2,1,0:T(1,128)}, u32[]{:S(2)}, u32[]{:S(2)}) async-start(f32[8,1,110592]{2,1,0:T(1,128)} %reshape.517), calls=%async_computation.3 | async-start | bytes 7077888 | tf_op jit(solution)/shard_map/all_to_all | solution.py:226
  505.6 14.6 %copy-start.7 = (f32[384,2304]{0,1:T(8,128)S(1)}, f32[384,2304]{0,1:T(8,128)}, u32[]{:S(2)}) copy-start(f32[384,2304]{0,1:T(8,128)} %reshape.480) | copy-start | bytes 10616836
  597.6 11.4 copy-start.8
  609.0 9.7 copy-start.13
  609.0 9.7 copy-start.14
  622.9 9.4 copy-start.9
  622.9 9.4 copy-start.11
  664.0 48.1 %all-to-all-start.4 = ((f32[8,1,110592]{2,1,0:T(1,128)}), f32[8,1,110592]{2,1,0:T(1,128)}, u32[]{:S(2)}, u32[]{:S(2)}) async-start(f32[8,1,110592]{2,1,0:T(1,128)} %reshape.519), calls=%async_computation.4 | async-start | bytes 7077888 | tf_op jit(solution)/shard_map/all_to_all | solution.py:245
  668.9 11.5 copy-start.10
  712.0 85.5 %all-to-all-start.5 = ((f32[8,1,110592]{2,1,0:T(1,128)}), f32[8,1,110592]{2,1,0:T(1,128)}, u32[]{:S(2)}, u32[]{:S(2)}) async-start(f32[8,1,110592]{2,1,0:T(1,128)} %reshape.521), calls=%async_computation.5 | async-start | bytes 7077888 | tf_op jit(solution)/shard_map/all_to_all | solution.py:246
  864.4 11.5 copy-start.12
  897.4 84.8 %all-to-all-start.6 = ((f32[4,1,221184]{2,1,0:T(1,128)}), f32[4,1,221184]{2,1,0:T(1,128)}, u32[]{:S(2)}, u32[]{:S(2)}) async-start(f32[4,1,221184]{2,1,0:T(1,128)} %reshape.523), calls=%async_computation.6 | async-start | bytes 7077888 | tf_op jit(solution)/shard_map/all_to_all | solution.py:250
  902.4 11.5 copy-start.4
  982.2 84.1 %all-to-all-start.7 = ((f32[4,1,221184]{2,1,0:T(1,128)}), f32[4,1,221184]{2,1,0:T(1,128)}, u32[]{:S(2)}, u32[]{:S(2)}) async-start(f32[4,1,221184]{2,1,0:T(1,128)} %reshape.525), calls=%async_computation.7 | async-start | bytes 7077888 | tf_op jit(solution)/shard_map/all_to_all | solution.py:251
  1132.1 11.1 copy-start.15
  1152.2 8.1 collective-permute-start.9
  1153.3 9.1 collective-permute-start.8
  1162.4 8.8 copy-start.17
  1162.4 8.8 copy-start.20
  1162.4 8.8 copy-start.23
  1162.5 8.7 collective-permute-start.11
  1164.0 7.2 collective-permute-start.10
  1171.3 7.5 copy-start.21
  1178.8 7.8 copy-start.22
  1178.8 7.9 copy-start.18
  1178.8 7.9 copy-start.29
  1178.8 8.4 copy-start.26
  1178.8 9.0 copy-start.1
  (7 other events, 26.7 us)
where the time goes:
time: 1200 us; the launch traced here: 1190 us
  local copies, waits for them, and re-layouts  368 us (31%)
  other arithmetic  268 us (22%)
  matrix products  247 us (21%)
  waiting for transfers between devices  245 us (20%)
  starting transfers between devices  57.6 us (5%)
    unnamed x16, matrix products  174 us
    unnamed x87, local copies, waits for them, and re-layouts  153 us
    all_to_all x1, waiting for transfers between devices, local(): lax.all_to_all(real_part, 'gy', split_axis=2, concat_axis=1, tiled=True)  90.8 us
    all_to_all x1, waiting for transfers between devices, local(): lax.all_to_all(imag_part, 'gy', split_axis=2, concat_axis=1, tiled=True)  82.3 us
    all_to_all x1, other arithmetic, local(): lax.all_to_all(imag_part, 'gy', split_axis=1, concat_axis=2, tiled=True)  40.7 us
    all_to_all x1, other arithmetic, local(): lax.all_to_all(real_part, 'gy', split_axis=1, concat_axis=2, tiled=True)  40.4 us
    all_to_all x1, other arithmetic, local(): lax.all_to_all(imag_part, 'gx', split_axis=1, concat_axis=0, tiled=True)  39.6 us
    all_to_all x1, other arithmetic, local(): lax.all_to_all(imag_part, 'gx', split_axis=0, concat_axis=1, tiled=True)  39.4 us
  transfers between devices with their start and end apart: 20, of which 9 were waited for; matrix products, arithmetic and copies ran while one was open for 35% of the time, Pallas kernels for 0%

commit v1 on v0

--- a/solution.py
+++ b/solution.py
@@ -3,17 +3,410 @@
 import jax
 import jax.numpy as jnp
 from jax import lax
+from jax.experimental import pallas as pl
+from jax.experimental.pallas import tpu as pltpu
 from jax.sharding import PartitionSpec as P
 
 GRID = 384
 AXIS = 16
-
+LANES = 128
+CHUNK = 512
+TILE = 256
 
 highest = lax.Precision.HIGHEST
 radius_scale = 4.0
 screen_width = 0.25
 norm_floor = 1e-06
 full_turn = 2.0 * math.pi
+
+
+def charge_kernel(nearby_ref, listed_ref, scale_ref, bias_ref, mixed_ref, env_ref):
+    neigh, atoms = listed_ref.shape
+    listed = listed_ref[...]
+    slot = listed % atoms
+    block = listed // atoms
+    square = jnp.zeros((neigh, atoms), jnp.float32)
+    deltas = []
+    for c in range(3):
+        center = nearby_ref[c, 4:5, :]
+        picked = jnp.zeros((neigh, atoms), jnp.float32)
+        for b in range(9):
+            row = jnp.broadcast_to(nearby_ref[c, b : b + 1, :], (neigh, atoms))
+            got = jnp.take_along_axis(row, slot, axis=1, mode="promise_in_bounds")
+            picked = jnp.where(block == b, got, picked)
+        delta = picked - center
+        deltas.append(delta)
+        square = square + delta * delta
+    radius = jnp.sqrt(square)
+    smooth = 1.0 / (1.0 + radius / radius_scale)
+    factor = smooth / (radius + radius_scale)
+    env_ref[0] = smooth
+    for c in range(3):
+        env_ref[c + 1] = deltas[c] * factor
+    mixed_ref[...] = jnp.zeros_like(mixed_ref)
+
+    def step(k, carry):
+        row = env_ref[0, pl.ds(k, 1), :]
+        embed = jnp.tanh(row * scale_ref[...] + bias_ref[...])
+        for c in range(4):
+            mixed_ref[c] += embed * env_ref[c, pl.ds(k, 1), :]
+        return carry
+
+    lax.fori_loop(0, neigh, step, 0)
+
+
+def mixed_features(nearby, listed, embed_scale, embed_bias):
+    neigh, atoms = listed.shape
+    width = embed_scale.shape[0]
+    spread = jnp.broadcast_to(embed_scale[:, None], (width, atoms))
+    shift = jnp.broadcast_to(embed_bias[:, None], (width, atoms))
+    return pl.pallas_call(
+        charge_kernel,
+        out_shape=jax.ShapeDtypeStruct((4, width, atoms), jnp.float32),
+        scratch_shapes=[pltpu.VMEM((4, neigh, atoms), jnp.float32)],
+    )(nearby, listed, spread, shift)
+
+
+def fit_charge(mixed, count, desc_gain, fit_in, fit_bias, fit_hidden, fit_bias_two, fit_out):
+    atoms = mixed.shape[2]
+    descriptor = jnp.sum(mixed[:, :, None, :] * mixed[:, None, :AXIS, :], axis=0).reshape(-1, atoms)
+    scaling = lax.rsqrt(jnp.mean(descriptor * descriptor, axis=0) + norm_floor)
+    normed = (descriptor * scaling[None, :] * desc_gain[:, None]).astype(jnp.bfloat16)
+    first = jnp.tanh(
+        jnp.dot(fit_in, normed, preferred_element_type=jnp.float32) + fit_bias[:, None]
+    )
+    second = (
+        jnp.tanh(
+            jnp.dot(fit_hidden, first.astype(jnp.bfloat16), preferred_element_type=jnp.float32)
+            + fit_bias_two[:, None]
+        )
+        + first
+    )
+    charge = jnp.sum(fit_out[:, None] * second, axis=0)
+    slot_index = lax.broadcasted_iota(jnp.int32, (atoms,), 0)
+    return jnp.where(slot_index < count, charge, jnp.zeros((), charge.dtype))
+
+
+def pack_kernel(count_ref, sites_ref, packed_ref):
+    columns, rows, atoms = sites_ref.shape
+    packed_ref[...] = jnp.zeros_like(packed_ref)
+    lane = lax.broadcasted_iota(jnp.int32, (rows, atoms), 1)
+
+    def step(j, start):
+        count = count_ref[j]
+        tile = start // atoms
+        shift = start % atoms
+        block = jnp.where(lane < count, sites_ref[j], 0.0)
+        turned = pltpu.roll(block, shift, 1)
+        packed_ref[tile] = packed_ref[tile] + jnp.where(lane >= shift, turned, 0.0)
+        packed_ref[tile + 1] = jnp.where(lane < shift, turned, 0.0)
+        return start + count
+
+    lax.fori_loop(0, columns, step, 0)
+
+
+def pack_sites(counts, sites):
+    columns, rows, atoms = sites.shape
+    return pl.pallas_call(
+        pack_kernel,
+        in_specs=[
+            pl.BlockSpec(memory_space=pltpu.SMEM),
+            pl.BlockSpec(memory_space=pltpu.VMEM),
+        ],
+        out_specs=pl.BlockSpec(memory_space=pltpu.VMEM),
+        out_shape=jax.ShapeDtypeStruct((columns + 1, rows, atoms), jnp.float32),
+    )(counts, sites)
+
+
+def axis_waves(cell, start, groups):
+    def turn(index):
+        angle = ((index * cell[None, :]) % GRID).astype(jnp.float32) * (full_turn / GRID)
+        return jnp.cos(angle), jnp.sin(angle)
+
+    low_cos, low_sin = turn(jnp.arange(8, dtype=jnp.int32)[:, None])
+    high_cos, high_sin = turn(start + 8 * jnp.arange(groups, dtype=jnp.int32)[:, None])
+    low_cos, low_sin = low_cos[None], low_sin[None]
+    high_cos, high_sin = high_cos[:, None], high_sin[:, None]
+    cosine = high_cos * low_cos - high_sin * low_sin
+    sine = high_sin * low_cos + high_cos * low_sin
+    return cosine.reshape(groups * 8, -1), sine.reshape(groups * 8, -1)
+
+
+def axis_table(cosine, sine, taps, start):
+    count = cosine.shape[0]
+    angle = (start + jnp.arange(count, dtype=jnp.int32)).astype(jnp.float32) * (full_turn / GRID)
+    angle = angle[:, None]
+    real = taps[1] + (taps[0] + taps[2]) * jnp.cos(angle) + taps[3] * jnp.cos(2.0 * angle)
+    imag = (taps[2] - taps[0]) * jnp.sin(angle) + taps[3] * jnp.sin(2.0 * angle)
+    return cosine * real - sine * imag, sine * real + cosine * imag
+
+
+def plane_tables(cell, taps, slopes, start, groups):
+    cosine, sine = axis_waves(cell, start, groups)
+    parity = (1 - 2 * (cell % 2)).astype(jnp.float32)
+    zero_mode = (start + jnp.arange(groups * 8, dtype=jnp.int32) == 0)[:, None]
+    tables = []
+    for row in (taps, slopes):
+        even, odd = axis_table(cosine, sine, row, start)
+        last = parity * (row[1] + row[3] - row[0] - row[2])
+        tables.append(jnp.concatenate([even, jnp.where(zero_mode, last[None], odd)], axis=0))
+    return tables
+
+
+def plane_modes(start, count):
+    mode = start + jnp.arange(count, dtype=jnp.int32)
+    modes = jnp.concatenate([mode, jnp.where(mode == 0, GRID // 2, mode)])
+    factor = jnp.where((modes == 0) | (modes == GRID // 2), 1.0, 2.0) / GRID
+    wave = modes.astype(jnp.float32) * (full_turn / GRID)
+    return wave * wave, factor.astype(jnp.float32)
+
+
+def halves(table):
+    high = lax.reduce_precision(table, 8, 7)
+    low = table - high
+    return jnp.concatenate([high, low], axis=0).astype(jnp.bfloat16)
+
+
+def mesh_kernel(
+    count_ref,
+    squares_ref,
+    factors_ref,
+    square_y_ref,
+    square_z_ref,
+    charge_ref,
+    x_ref,
+    slope_x_ref,
+    y_ref,
+    slope_y_ref,
+    z_ref,
+    slope_z_ref,
+    out_ref,
+    spectrum_ref,
+    scaled_ref,
+    found_ref,
+):
+    modes_x = x_ref.shape[0]
+    modes_y = y_ref.shape[0]
+    depth = z_ref.shape[0]
+    modes_z = depth // 2
+    columns = out_ref.shape[0]
+    group = 8
+    total = lax.fori_loop(0, columns, lambda j, acc: acc + count_ref[j], 0)
+    spectrum_ref[...] = jnp.zeros_like(spectrum_ref)
+
+    def gather_chunk(chunk, carry):
+        lanes = pl.ds(pl.multiple_of(chunk * CHUNK, CHUNK), CHUNK)
+        y = y_ref[:, lanes] * charge_ref[:, lanes]
+        high = z_ref[:modes_z, lanes]
+        low = z_ref[modes_z:, lanes]
+
+        def rows(g, inner):
+            x = x_ref[pl.ds(pl.multiple_of(g * group, group), group), lanes]
+            left = jnp.concatenate(
+                [(x[a : a + 1] * y).astype(jnp.bfloat16) for a in range(group)], axis=0
+            )
+            where = pl.ds(pl.multiple_of(g * group * modes_y, group * modes_y), group * modes_y)
+            form = (((1,), (1,)), ((), ()))
+            spectrum_ref[where, :] += lax.dot_general(
+                left, high, form, preferred_element_type=jnp.float32
+            ) + lax.dot_general(left, low, form, preferred_element_type=jnp.float32)
+            return inner
+
+        return lax.fori_loop(0, modes_x // group, rows, carry)
+
+    lax.fori_loop(0, (total + CHUNK - 1) // CHUNK, gather_chunk, 0)
+
+    square_y = square_y_ref[:, 0:1]
+    factor_y = square_y_ref[:, 1:2]
+    square_z = square_z_ref[0:1, :]
+    factor_z = square_z_ref[1:2, :]
+    plane = square_y + square_z
+    weight = factor_y * factor_z * (2.0 * full_turn)
+
+    def scale(a, carry):
+        square = plane + squares_ref[a]
+        safe = jnp.where(square > 0, square, 1.0)
+        green = jnp.exp(square * (-0.5 * screen_width * screen_width)) / safe
+        green = jnp.where(square > 0, green, 0.0) * (weight * factors_ref[a])
+        where = pl.ds(pl.multiple_of(a * modes_y, modes_y), modes_y)
+        value = (spectrum_ref[where, :] * green).astype(jnp.bfloat16)
+        scaled_ref[where, :modes_z] = value
+        scaled_ref[where, modes_z:] = value
+        return carry
+
+    lax.fori_loop(0, modes_x, scale, 0)
+    found_ref[...] = jnp.zeros_like(found_ref)
+
+    def tile_step(tile, carry):
+        lanes = pl.ds(pl.multiple_of(tile * TILE, TILE), TILE)
+        y = y_ref[:, lanes]
+        slope_y = slope_y_ref[:, lanes]
+        z = z_ref[:, lanes]
+        slope_z = slope_z_ref[:, lanes]
+
+        def rows(g, sums):
+            spot = pl.ds(pl.multiple_of(g * group, group), group)
+            x = x_ref[spot, lanes]
+            slope_x = slope_x_ref[spot, lanes]
+            where = pl.ds(pl.multiple_of(g * group * modes_y, group * modes_y), group * modes_y)
+            left = scaled_ref[where, :]
+            along = jnp.dot(left, z, preferred_element_type=jnp.float32)
+            slant = jnp.dot(left, slope_z, preferred_element_type=jnp.float32)
+            value, field_x, field_y, field_z = sums
+            for a in range(group):
+                part = along[a * modes_y : (a + 1) * modes_y]
+                skew = slant[a * modes_y : (a + 1) * modes_y]
+                over = jnp.sum((part * y).reshape(modes_y // 8, 8, TILE), axis=0)
+                tilt = jnp.sum((part * slope_y).reshape(modes_y // 8, 8, TILE), axis=0)
+                deep = jnp.sum((skew * y).reshape(modes_y // 8, 8, TILE), axis=0)
+                row = x[a : a + 1]
+                value = value + over * row
+                field_x = field_x + over * slope_x[a : a + 1]
+                field_y = field_y + tilt * row
+                field_z = field_z + deep * row
+            return value, field_x, field_y, field_z
+
+        zero = jnp.zeros((8, TILE), jnp.float32)
+        sums = lax.fori_loop(0, modes_x // group, rows, (zero, zero, zero, zero))
+        for part in range(TILE // LANES):
+            for c in range(4):
+                found_ref[tile * (TILE // LANES) + part, c : c + 1, :] = jnp.sum(
+                    sums[c][:, part * LANES : (part + 1) * LANES], axis=0, keepdims=True
+                )
+        return carry
+
+    lax.fori_loop(0, (total + TILE - 1) // TILE, tile_step, 0)
+    lane = lax.broadcasted_iota(jnp.int32, (8, LANES), 1)
+
+    def place(j, start):
+        tile = start // LANES
+        shift = start % LANES
+        back = (LANES - shift) % LANES
+        first = pltpu.roll(found_ref[tile], back, 1)
+        second = pltpu.roll(found_ref[tile + 1], back, 1)
+        out_ref[j] = jnp.where(lane < LANES - shift, first, second)
+        return start + count_ref[j]
+
+    lax.fori_loop(0, columns, place, 0)
+
+
+def mesh_sums(counts, squares_x, factors_x, side_y, side_z, charge, tables):
+    columns = counts.shape[0]
+    modes_x = tables[0].shape[0]
+    modes_y = tables[2].shape[0]
+    modes_z = tables[4].shape[0] // 2
+    vmem = pl.BlockSpec(memory_space=pltpu.VMEM)
+    smem = pl.BlockSpec(memory_space=pltpu.SMEM)
+    return pl.pallas_call(
+        mesh_kernel,
+        in_specs=[smem, smem, smem] + [vmem] * 9,
+        out_specs=vmem,
+        out_shape=jax.ShapeDtypeStruct((columns, 8, LANES), jnp.float32),
+        scratch_shapes=[
+            pltpu.VMEM((modes_x * modes_y, modes_z), jnp.float32),
+            pltpu.VMEM((modes_x * modes_y, 2 * modes_z), jnp.bfloat16),
+            pltpu.VMEM((tables[0].shape[1] // LANES + 2, 8, LANES), jnp.float32),
+        ],
+        compiler_params=pltpu.CompilerParams(vmem_limit_bytes=60 * 2**20),
+    )(counts, squares_x, factors_x, side_y, side_z, charge, *tables)
+
+
+def local_sites(
+    positions,
+    neighbours,
+    live_count,
+    stencil_base,
+    spline_weight,
+    spline_slope,
+    embed_scale,
+    embed_bias,
+    desc_gain,
+    fit_in,
+    fit_bias,
+    fit_hidden,
+    fit_bias_two,
+    fit_out,
+):
+    both = ("gx", "gy")
+    columns_x = lax.axis_size("gx")
+    columns_y = lax.axis_size("gy")
+    columns = columns_x * columns_y
+    place_x = lax.axis_index("gx")
+    place_y = lax.axis_index("gy")
+    width_x = GRID // columns_x
+    width_y = GRID // columns_y
+    atoms = positions.shape[3]
+    origin = jnp.stack([place_x * width_x, place_y * width_y, 0])
+    cells = (stencil_base[:, 0, 0, :] + origin[:, None] + 1).astype(jnp.float32)
+    counted = jnp.broadcast_to(live_count.astype(jnp.float32), (1, atoms))
+    parcel = jnp.concatenate(
+        [
+            positions[:, 0, 0, :],
+            counted,
+            cells,
+            spline_weight[:, :, 0, 0, :].reshape(12, atoms),
+            spline_slope[:, :, 0, 0, :].reshape(12, atoms),
+        ],
+        axis=0,
+    )
+    shared = lax.all_gather(parcel, both, axis=0, tiled=False)
+    counts = shared[:, 3, 0].astype(jnp.int32)
+    near = []
+    for stride_x in (-1, 0, 1):
+        for stride_y in (-1, 0, 1):
+            other_x = (place_x + stride_x) % columns_x
+            other_y = (place_y + stride_y) % columns_y
+            block = lax.dynamic_index_in_dim(
+                shared, other_x * columns_y + other_y, axis=0, keepdims=False
+            )[:3]
+            offset = jnp.array([stride_x * width_x, stride_y * width_y, 0], jnp.float32)
+            near.append(block + offset[:, None])
+    mixed = mixed_features(
+        jnp.stack(near, axis=1), neighbours[:, 0, 0, :], embed_scale, embed_bias
+    )
+    charge = fit_charge(
+        mixed, live_count[0, 0], desc_gain, fit_in, fit_bias, fit_hidden, fit_bias_two, fit_out
+    )
+    charges = lax.all_gather(charge, both, axis=0, tiled=False)
+    sites = jnp.concatenate(
+        [shared[:, 4:], charges[:, None, :], jnp.zeros((columns, 4, atoms), jnp.float32)], axis=1
+    )
+    packed = pack_sites(counts, sites)[:columns]
+    slots = -(-(columns * atoms) // CHUNK) * CHUNK
+    packed = jnp.transpose(packed, (1, 0, 2)).reshape(packed.shape[1], columns * atoms)
+    packed = jnp.pad(packed, ((0, 0), (0, slots - columns * atoms)))
+    cells = packed[:3].astype(jnp.int32)
+    taps = packed[3:15].reshape(3, 4, -1)
+    slopes = packed[15:27].reshape(3, 4, -1)
+    half_x = GRID // columns_x // 2
+    half_y = GRID // columns_y // 2
+    start_x = place_x * half_x
+    start_y = place_y * half_y
+    table_x, slope_x = plane_tables(cells[0], taps[0], slopes[0], start_x, half_x // 8)
+    table_y, slope_y = plane_tables(cells[1], taps[1], slopes[1], start_y, half_y // 8)
+    cosine, sine = axis_waves(cells[2], 0, GRID // 16)
+    table_z = halves(jnp.concatenate(axis_table(cosine, sine, taps[2], 0), axis=0))
+    slope_z = halves(jnp.concatenate(axis_table(cosine, sine, slopes[2], 0), axis=0))
+    squares_x, factors_x = plane_modes(start_x, half_x)
+    squares_y, factors_y = plane_modes(start_y, half_y)
+    mode_z = jnp.arange(GRID, dtype=jnp.int32) % (GRID // 2)
+    wave_z = mode_z.astype(jnp.float32) * (full_turn / GRID)
+    factors_z = jnp.where(mode_z == 0, 1.0, 2.0).astype(jnp.float32) / GRID
+    side_y = jnp.stack([squares_y, factors_y], axis=1)
+    side_z = jnp.stack([wave_z * wave_z, factors_z], axis=0)
+    sums = mesh_sums(
+        counts,
+        squares_x,
+        factors_x,
+        side_y,
+        side_z,
+        packed[27:28],
+        (table_x, slope_x, table_y, slope_y, table_z, slope_z),
+    )
+    mine = lax.psum_scatter(sums[:, :4], both, scatter_dimension=0, tiled=True)[0]
+    energy = (0.5 * charge * mine[0]).reshape(1, 1, atoms)
+    force = (-charge[None, :] * mine[1:]).reshape(3, 1, 1, atoms)
+    return (energy, force)
 
 
 def padded_2(shard, sides, width):
@@ -149,7 +542,7 @@
     return (real_cos + sign * imag_sin, imag_cos - sign * real_sin)
 
 
-def local(
+def local_mesh(
     positions,
     neighbours,
     live_count,
@@ -267,6 +660,13 @@
 
 
 def solution(mesh):
+    def local(positions, *rest):
+        columns_x, columns_y = (lax.axis_size("gx"), lax.axis_size("gy"))
+        sites = columns_x * columns_y * positions.shape[3]
+        whole = GRID % (16 * columns_x) == 0 and GRID % (16 * columns_y) == 0
+        few = whole and sites <= 8 * GRID * 2
+        return (local_sites if few and positions.shape[3] == LANES else local_mesh)(positions, *rest)
+
     placed = (
         P(None, "gx", "gy", None),
         P(None, "gx", "gy", None),

time: 1200 us -> 409 us (0.34)
  local copies, waits for them, and re-layouts: 368 us -> 12 us
  matrix products: 247 us -> 0.52 us
  other arithmetic: 268 us -> 44.7 us
  blocking collectives: 0 us -> 138 us
  waiting for transfers between devices: 245 us -> 118 us
  Pallas kernels: 0 us -> 79.6 us
  starting transfers between devices: 57.6 us -> 0.04 us
  between operations: 2.51 us -> 15.6 us
    all_to_all x6 -> x0, other arithmetic: 239 us -> none  [the longest x1 40.7 us: local(): lax.all_to_all(imag_part, 'gy', split_axis=1, concat_axis=2, tiled=True)]
    all_to_all x8 -> x0, waiting for transfers between devices: 224 us -> none  [the longest x1 90.8 us: local(): lax.all_to_all(real_part, 'gy', split_axis=2, concat_axis=1, tiled=True)]
    unnamed x16 -> x0, matrix products: 174 us -> none
    unnamed x87 -> x106, local copies, waits for them, and re-layouts: 153 us -> 3.53 us
    all_gather x0 -> x2, blocking collectives: none -> 138 us  [the longest x1 74.1 us: local_sites(): shared = lax.all_gather(parcel, both, axis=0, tiled=False)]
    unnamed x0 -> x2, waiting for transfers between devices: none -> 118 us
    all_to_all x13 -> x0, local copies, waits for them, and re-layouts: 100 us -> none  [the longest x2 18 us: local(): lax.all_to_all(imag_part, 'gx', split_axis=0, concat_axis=1, tiled=True)]
    pallas_call x0 -> x3, Pallas kernels: none -> 79.6 us  [the longest x1 72.4 us: mesh_sums(): pl.pallas_call(mesh_kernel, in_specs=[smem, smem, smem] + [vmem] * 9, out...]
  transfers between devices with their start and end apart: 20 -> 1, of which waited for: 9 -> 1; matrix products, arithmetic and copies ran while one was open for 35% -> 0% of each run, Pallas kernels for 0% -> 0%
where the time goes in v1:
time: 409 us; the launch traced here: 408 us
  blocking collectives  138 us (34%)
  waiting for transfers between devices  118 us (29%)
  Pallas kernels  79.6 us (19%)
  other arithmetic  44.7 us (11%)
  between operations  15.6 us (4%)
  local copies, waits for them, and re-layouts  12 us (3%)
    unnamed x2, waiting for transfers between devices  118 us
    all_gather x1, blocking collectives, local_sites(): shared = lax.all_gather(parcel, both, axis=0, tiled=False)  74.1 us
    pallas_call x1, Pallas kernels, mesh_sums(): pl.pallas_call(mesh_kernel, in_specs=[smem, smem, smem] + [vmem] * 9, out...  72.4 us
    all_gather x1, blocking collectives, local_sites(): charges = lax.all_gather(charge, both, axis=0, tiled=False)  63.4 us
  transfers between devices with their start and end apart: 1, of which 1 were waited for; matrix products, arithmetic and copies ran while one was open for 0% of the time, Pallas kernels for 0%

profile of v1, /device:TPU:0, one launch (start us, length us, event | category | flops | bytes accessed | tf_op | source)
XLA Modules:
  0.0 407.6 jit_solution(9175539223673196817)
XLA Ops:
  8.0 0.7 pad.91
  8.7 0.7 pad.92
  9.4 0.7 copy.110
  10.2 0.8 fusion.78
  11.2 74.1 %all-gather.1 = f32[32,31,128]{2,1,0:T(8,128)S(1)} all-gather(f32[1,31,128]{2,1,0:T(8,128)S(1)} %bitcast.253), channel_id=2, replica_groups=mesh['gx'=8,'gy'=4] {'gx','gy'}, dimensions={0}, use_global_device_ids=true | all-gather | bytes 523776 | tf_op jit(solution)/shard_map/all_gather | solution.py:352
  85.3 1.2 fusion.76.count_ref
  86.5 0.7 fusion.80
  87.3 0.7 fusion.82
  88.0 0.7 fusion.84
  88.8 0.7 fusion.86
  89.5 1.2 stack.15.nearby_ref
  90.7 1.4 broadcast_in_dim.101.scale_ref
  92.1 1.4 broadcast_in_dim.104.bias_ref
  93.5 2.9 shard_map.230
  96.4 0.8 slice.339
  97.2 1.3 multiply_reduce_fusion
  99.6 63.4 %all-gather.2 = f32[32,1,128]{2,1,0:T(1,128)S(1)} all-gather(f32[1,1,128]{2,1,0:T(1,128)S(1)} %fusion.96), channel_id=1, replica_groups=mesh['gx'=8,'gy'=4] {'gx','gy'}, dimensions={0}, use_global_device_ids=true | all-gather | bytes 16896 | tf_op jit(solution)/shard_map/all_gather | solution.py:370
  163.1 0.9 maximum_maximum_fusion.sites_ref
  164.1 4.3 %shard_map.231 = f32[33,32,128]{2,1,0:T(8,128)} custom-call(s32[32]{0:T(128)} %fusion.76.count_ref, f32[32,32,128]{2,1,0:T(8,128)} %maximum_maximum_fusion.sites_ref), custom_call_target="tpu_custom_call" | custom-call | tf_op jit(solution)/shard_map/pallas_call | solution.py:110
  168.3 1.1 slice_bitcast_fusion
  169.4 0.8 fusion.110
  170.4 0.8 bitcast_multiply_fusion.25
  171.2 0.9 fusion.111
  172.1 0.6 fusion.100
  173.8 0.6 fusion.104
  174.4 0.6 fusion.106
  177.3 1.7 fusion.30
  178.9 1.2 fusion.47
  180.2 1.3 fusion.51
  181.5 1.2 fusion.55
  182.7 1.2 fusion.66
  184.0 0.7 copy.53.square_y_ref
  184.8 3.7 fusion.4
  188.5 1.3 reduce-precision_convert_fusion
  189.8 3.5 pad_maximum_fusion.3.slope_z_ref
  193.3 1.2 reduce-precision_convert_fusion.1
  194.7 3.4 pad_maximum_fusion.1.z_ref
  198.2 1.5 bitcast_multiply_fusion.26
  199.9 0.9 fusion.13
  201.0 1.3 pad_maximum_fusion.5.slope_y_ref
  202.3 1.3 pad_maximum_fusion.4.y_ref
  204.2 0.9 pad_maximum_fusion.7.slope_x_ref
  205.2 1.0 pad_maximum_fusion.6.x_ref
  206.1 0.7 fusion.94
  207.4 72.4 %shard_map.232 = f32[32,8,128]{2,1,0:T(8,128)} custom-call(s32[32]{0:T(128)} %fusion.76.count_ref, f32[48]{0:T(128)} %get-tuple-element.92.squares_ref, f32[48]{0:T(128)} %get-tuple-element.91.factors_ref, f32[96,2]{1,0:T(8,128)} %copy.53.square_y_ref, f32[2,384]{1,0:T(2,128)} %pad_maximum_fusion.8.square_z_ref, f32[1,4096]{1,0:T(1,128)} %get-tuple-element.56.charge_ref, ...), custom_call_target="tpu_custom_call" | custom-call | tf_op jit(solution)/shard_map/pallas_call | solution.py:300
  279.8 1.5 slice.372
  281.3 117.6 %all-reduce.3.cloned.1.call-done = f32[32,4,128]{2,1,0:T(4,128)} async-done(((f32[32,4,128]{2,1,0:T(4,128)}), f32[32,4,128]{2,1,0:T(4,128)}) %all-reduce.3.cloned.1.call-update) | async-done | bytes 65552
  399.0 0.7 constant_dynamic-slice_fusion.9
  (138 shorter events, 7.5 us)
Async XLA Ops:
  7.2 91.8 %copy-start = (bf16[128,1600]{0,1:T(8,128)(2,1)S(1)}, bf16[128,1600]{0,1:T(8,128)(2,1)}, u32[]{:S(2)}) copy-start(bf16[128,1600]{0,1:T(8,128)(2,1)} %param.32) | copy-start | bytes 1228804
  7.2 91.5 %copy-start.28 = (f32[1600]{0:T(1024)S(1)}, f32[1600]{0:T(1024)}, u32[]{:S(2)}) copy-start(f32[1600]{0:T(1024)} %param.31) | copy-start | bytes 19204
  7.2 91.8 %copy-start.31 = (f32[128]{0:T(128)S(1)}, f32[128]{0:T(128)}, u32[]{:S(2)}) copy-start(f32[128]{0:T(128)} %param.33) | copy-start | bytes 1540
  7.2 391.8 %all-reduce.3.cloned.1.call-start = ((), (), s32[]{:S(2)}) async-start(), calls=%async_computation | async-start | bytes 131072
  11.2 88.2 %copy-start.46 = (bf16[128,128]{1,0:T(8,128)(2,1)S(1)}, bf16[128,128]{1,0:T(8,128)(2,1)}, u32[]{:S(2)}) copy-start(bf16[128,128]{1,0:T(8,128)(2,1)} %param.34) | copy-start | bytes 98308
  11.2 88.2 %copy-start.47 = (f32[128]{0:T(128)S(1)}, f32[128]{0:T(128)}, u32[]{:S(2)}) copy-start(f32[128]{0:T(128)} %param.35) | copy-start | bytes 1540
  11.2 88.2 %copy-start.48 = (f32[128]{0:T(128)S(1)}, f32[128]{0:T(128)}, u32[]{:S(2)}) copy-start(f32[128]{0:T(128)} %param.36) | copy-start | bytes 1540
  99.6 63.5 %copy-start.37 = (f32[128]{0:T(128)}, f32[128]{0:T(128)S(1)}, u32[]{:S(2)}) copy-start(f32[128]{0:T(128)S(1)} %fusion.10) | copy-start | bytes 1540
  169.4 19.1 %copy-start.1 = (f32[32,32,128]{2,0,1:T(8,128)}, f32[32,32,128]{2,0,1:T(8,128)S(1)}, u32[]{:S(2)}) copy-start(f32[32,32,128]{2,0,1:T(8,128)S(1)} %slice_bitcast_fusion) | copy-start | bytes 1572868
  194.5 3.6 copy-start.26
  194.5 3.6 copy-start.27
  194.6 5.2 %copy-start.4 = (f32[8,4096]{1,0:T(8,128)S(1)}, f32[8,4096]{1,0:T(8,128)}, u32[]{:S(2)}) copy-start(f32[8,4096]{1,0:T(8,128)} %get-tuple-element.85) | copy-start | bytes 393220
  194.6 5.2 %copy-start.5 = (f32[8,4096]{1,0:T(8,128)S(1)}, f32[8,4096]{1,0:T(8,128)}, u32[]{:S(2)}) copy-start(f32[8,4096]{1,0:T(8,128)} %get-tuple-element.86) | copy-start | bytes 393220
  194.6 5.2 %copy-start.6 = (f32[6,4096]{1,0:T(8,128)S(1)}, f32[6,4096]{1,0:T(8,128)}, u32[]{:S(2)}) copy-start(f32[6,4096]{1,0:T(8,128)} %get-tuple-element.79) | copy-start | bytes 294916
  194.6 5.2 %copy-start.7 = (f32[6,4096]{1,0:T(8,128)S(1)}, f32[6,4096]{1,0:T(8,128)}, u32[]{:S(2)}) copy-start(f32[6,4096]{1,0:T(8,128)} %get-tuple-element.80) | copy-start | bytes 294916
  194.6 5.2 %copy-start.9 = (f32[1,4096]{1,0:T(1,128)S(1)}, f32[1,4096]{1,0:T(1,128)}, u32[]{:S(2)}) copy-start(f32[1,4096]{1,0:T(1,128)} %get-tuple-element.10) | copy-start | bytes 49156
  194.6 5.2 %copy-start.18 = (f32[1,32,128]{2,0,1:T(1,128)S(1)}, f32[1,32,128]{2,0,1:T(1,128)}, u32[]{:S(2)}) copy-start(f32[1,32,128]{2,0,1:T(1,128)} %get-tuple-element.45) | copy-start | bytes 49156
  194.6 5.2 %copy-start.19 = (f32[1,32,128]{2,0,1:T(1,128)S(1)}, f32[1,32,128]{2,0,1:T(1,128)}, u32[]{:S(2)}) copy-start(f32[1,32,128]{2,0,1:T(1,128)} %get-tuple-element.46) | copy-start | bytes 49156
  194.6 5.2 %copy-start.20 = (f32[1,32,128]{2,0,1:T(1,128)S(1)}, f32[1,32,128]{2,0,1:T(1,128)}, u32[]{:S(2)}) copy-start(f32[1,32,128]{2,0,1:T(1,128)} %get-tuple-element.47) | copy-start | bytes 49156
  194.6 5.2 %copy-start.21 = (f32[1,32,128]{2,0,1:T(1,128)S(1)}, f32[1,32,128]{2,0,1:T(1,128)}, u32[]{:S(2)}) copy-start(f32[1,32,128]{2,0,1:T(1,128)} %get-tuple-element.40) | copy-start | bytes 49156
  194.6 5.2 %copy-start.22 = (f32[1,32,128]{2,0,1:T(1,128)S(1)}, f32[1,32,128]{2,0,1:T(1,128)}, u32[]{:S(2)}) copy-start(f32[1,32,128]{2,0,1:T(1,128)} %get-tuple-element.41) | copy-start | bytes 49156
  194.7 5.2 %copy-start.23 = (f32[1,32,128]{2,0,1:T(1,128)S(1)}, f32[1,32,128]{2,0,1:T(1,128)}, u32[]{:S(2)}) copy-start(f32[1,32,128]{2,0,1:T(1,128)} %get-tuple-element.42) | copy-start | bytes 49156
  194.7 5.2 %copy-start.24 = (f32[1,32,128]{2,0,1:T(1,128)S(1)}, f32[1,32,128]{2,0,1:T(1,128)}, u32[]{:S(2)}) copy-start(f32[1,32,128]{2,0,1:T(1,128)} %get-tuple-element.43) | copy-start | bytes 49156
  194.7 5.2 %copy-start.25 = (f32[1,32,128]{2,0,1:T(1,128)S(1)}, f32[1,32,128]{2,0,1:T(1,128)}, u32[]{:S(2)}) copy-start(f32[1,32,128]{2,0,1:T(1,128)} %get-tuple-element.44) | copy-start | bytes 49156
  194.7 5.2 %copy-start.32 = (f32[48]{0:T(128)S(1)}, f32[48]{0:T(128)}, u32[]{:S(2)}) copy-start(f32[48]{0:T(128)} %get-tuple-element.111) | copy-start | bytes 580
  194.7 5.2 %copy-start.33 = (f32[48]{0:T(128)S(1)}, f32[48]{0:T(128)}, u32[]{:S(2)}) copy-start(f32[48]{0:T(128)} %get-tuple-element.112) | copy-start | bytes 580
  194.7 5.2 %copy-start.34 = (f32[48]{0:T(128)S(1)}, f32[48]{0:T(128)}, u32[]{:S(2)}) copy-start(f32[48]{0:T(128)} %get-tuple-element.113) | copy-start | bytes 580
  194.7 5.2 %copy-start.35 = (f32[48]{0:T(128)S(1)}, f32[48]{0:T(128)}, u32[]{:S(2)}) copy-start(f32[48]{0:T(128)} %get-tuple-element.114) | copy-start | bytes 580
  194.7 5.2 %copy-start.36 = (pred[48]{0:T(512)(128)(4,1)S(1)}, pred[48]{0:T(512)(128)(4,1)}, u32[]{:S(2)}) copy-start(pred[48]{0:T(512)(128)(4,1)} %fusion.98) | copy-start | bytes 148
  200.8 2.7 copy-start.2
  200.8 2.7 copy-start.3
  200.9 2.7 copy-start.8
  200.9 2.7 copy-start.10
  200.9 2.7 copy-start.11
  200.9 2.7 copy-start.12
  200.9 2.7 copy-start.13
  200.9 2.7 copy-start.14
  200.9 2.7 copy-start.15
  200.9 2.7 copy-start.16
  200.9 2.7 copy-start.17
  200.9 2.7 copy-start.41
  201.0 2.7 copy-start.42
  201.0 2.7 copy-start.43
  201.0 2.7 copy-start.44
  201.0 2.7 copy-start.45
  203.5 3.2 copy-start.29
  203.5 3.2 copy-start.30
  207.4 74.0 %copy-start.38 = (f32[128]{0:T(128)S(1)}, f32[128]{0:T(128)}, u32[]{:S(2)}) copy-start(f32[128]{0:T(128)} %copy-done.37) | copy-start | bytes 1540
  (2 other events, 5.2 us)
Sparse Core Ops, SparseCore 0:
  281.4 117.4 all-reduce.2
